TPU v7x, 512 devices: a whole 4x8x8 slice. The times are simulated.
512 devices in a mesh: dp: 128 (over y, z, core), mp: 4 (over x).
Axes of the slice: x: 4, y: 8, z: 8, core: 2. Of those that a mesh axis runs over, the one named last changes fastest.
Arguments:
- frames: bfloat16 [32768, 1024], P('dp'), may hold values from -24 to 24
- proj_in: bfloat16 [1024, 2, 1024], P(None, None, 'mp'), may hold values from -0.1875 to 0.1875
- depthwise: float32 [31, 1024], P(None, 'mp'), may hold values from -1 to 1
- bn_gain: float32 [1024], P('mp'), may hold values from 0.5 to 1.5
- bn_shift: float32 [1024], P('mp'), may hold values from -3 to 3
- proj_out: bfloat16 [1024, 1024], P(None, 'mp'), may hold values from -0.1875 to 0.1875
- grad_out: bfloat16 [32768, 1024], P('dp'), may hold values from -24 to 24
- counts: int32 [128], replicated, may hold values from 1 to 2, as said below
- lengths: int32 [128, 2], P('dp'), may hold values from 1 to 255, as said below
Outputs:
- frame_grad: bfloat16 [32768, 1024], P('dp', 'mp')
- in_grad: float32 [1024, 2, 1024], P('dp', None, 'mp')
- out_grad: float32 [1024, 1024], P('dp', 'mp')
- depth_grad: float32 [31, 1024], P(None, 'mp')
- gain_grad: float32 [1024], P('mp')
- shift_grad: float32 [1024], P('mp')
Inputs may be any that keep to these rules, and one draw needn't show every extreme that they name: `counts`: some device holds 2 live blocks. lengths[d] sums to 128 * counts[d]; on some device with 2 live blocks one utterance holds all frames but one for each other utterance.
All inputs are finite; a program needn't handle non-finite values.
Results may differ from a plain program's by a relative error of at most 0.0095.
Values may be sent and summed in bfloat16 or wider, within the bound.
No kernel may reach another device: no remote copies, remote signals or barrier semaphores. Data moves between devices by JAX's collectives and lax.ppermute only.
A program may use at most 64 MiB of HBM per device.

v0:
```python
import jax
import jax.numpy as jnp
from jax import lax
from jax.sharding import PartitionSpec as P

BLOCK = 128


def time_shift(values, offset, fill_value):
    if offset > 0:
        pad_part = jnp.full((offset,) + values.shape[1:], fill_value, values.dtype)
        return jnp.concatenate([values[offset:], pad_part], axis=0)
    if offset < 0:
        pad_part = jnp.full((-offset,) + values.shape[1:], fill_value, values.dtype)
        return jnp.concatenate([pad_part, values[:offset]], axis=0)
    return values


def tap_term(glu_float, owner_id, live_col, offset):
    same_utt = (time_shift(owner_id, offset, -1) == owner_id).astype(jnp.float32)[
        :, None
    ] * live_col
    return time_shift(glu_float, offset, 0.0) * same_utt


def shards(frames, proj_in, depthwise, bn_gain, bn_shift, proj_out, grad_out, counts, lengths):
    frames_dev = frames.shape[0]
    model_width = frames.shape[1]
    channels = proj_in.shape[2]
    tap_count = depthwise.shape[0]
    radius = tap_count // 2
    rows_dev = model_width // lax.axis_size("dp")
    position = jnp.arange(frames_dev, dtype=jnp.int32)
    utt_ends = jnp.cumsum(lengths[0])
    owner_id = jnp.sum((position[:, None] >= utt_ends[None, :]).astype(jnp.int32), axis=1)
    my_count = counts[lax.axis_index("dp")]
    live_col = (position < my_count * BLOCK).astype(jnp.float32)[:, None]
    frame_total = (jnp.sum(counts) * BLOCK).astype(jnp.float32)
    proj_flat = proj_in.reshape(model_width, 2 * channels)
    pre_act = jnp.dot(frames, proj_flat, preferred_element_type=jnp.float32)
    value_half = pre_act[:, :channels]
    gate_sig = jax.nn.sigmoid(pre_act[:, channels:])
    glu_out = (value_half * gate_sig * live_col).astype(jnp.bfloat16)
    glu_float = lax.optimization_barrier(glu_out).astype(jnp.float32)
    conv_out = jnp.zeros((frames_dev, channels), jnp.float32)
    for tap_index in range(tap_count):
        conv_out = conv_out + depthwise[tap_index] * tap_term(
            glu_float, owner_id, live_col, tap_index - radius
        )
    sum_val, sum_sq = lax.psum(
        (jnp.sum(conv_out, axis=0), jnp.sum(conv_out * conv_out, axis=0)), "dp"
    )
    mean_val = sum_val / frame_total
    square_mean = sum_sq / frame_total
    inv_std = lax.rsqrt(square_mean - mean_val * mean_val + 1e-05)
    normed = (conv_out - mean_val) * inv_std
    scaled = normed * bn_gain + bn_shift
    sig_scaled = jax.nn.sigmoid(scaled)
    hidden = (scaled * sig_scaled * live_col).astype(jnp.bfloat16)
    grad_hidden = jnp.dot(grad_out, proj_out, preferred_element_type=jnp.float32) * live_col
    grad_scaled = grad_hidden * sig_scaled * (1.0 + scaled * (1.0 - sig_scaled))
    local_shift = jnp.sum(grad_scaled, axis=0)
    local_gain = jnp.sum(grad_scaled * normed, axis=0)
    shift_grad, gain_grad = lax.psum((local_shift, local_gain), "dp")
    grad_conv = (
        live_col
        * bn_gain
        * inv_std
        * (grad_scaled - shift_grad / frame_total - normed * gain_grad / frame_total)
    )
    depth_rows = []
    for tap_index in range(tap_count):
        depth_rows.append(
            jnp.sum(grad_conv * tap_term(glu_float, owner_id, live_col, tap_index - radius), axis=0)
        )
    depth_grad = lax.psum(jnp.stack(depth_rows), "dp")
    grad_glu = jnp.zeros((frames_dev, channels), jnp.float32)
    for tap_index in range(tap_count):
        offset = tap_index - radius
        back_same = (time_shift(owner_id, -offset, -1) == owner_id).astype(jnp.float32)[
            :, None
        ] * live_col
        grad_glu = grad_glu + depthwise[tap_index] * time_shift(grad_conv, -offset, 0.0) * back_same
    grad_value = grad_glu * gate_sig
    grad_gate = grad_glu * value_half * gate_sig * (1.0 - gate_sig)
    grad_flat = jnp.concatenate([grad_value, grad_gate], axis=1).astype(jnp.bfloat16)
    frame_term = lax.dot_general(
        grad_flat, proj_flat, (((1,), (1,)), ((), ())), preferred_element_type=jnp.float32
    )
    frame_grad = lax.psum_scatter(
        frame_term.astype(jnp.bfloat16), "mp", scatter_dimension=1, tiled=True
    )
    summed = lax.psum_scatter(
        jnp.concatenate(
            [
                lax.dot_general(
                    frames, grad_flat, (((0,), (0,)), ((), ())), preferred_element_type=jnp.float32
                ),
                lax.dot_general(
                    grad_out, hidden, (((0,), (0,)), ((), ())), preferred_element_type=jnp.float32
                ),
            ],
            axis=1,
        ),
        "dp",
        scatter_dimension=0,
        tiled=True,
    )
    in_flat = summed[:, : 2 * channels]
    out_grad = summed[:, 2 * channels :]
    in_grad = in_flat.reshape(rows_dev, 2, channels)
    return (frame_grad, in_grad, out_grad, depth_grad, gain_grad, shift_grad)


def solution(mesh):
    placed = (
        P("dp", None),
        P(None, None, "mp"),
        P(None, "mp"),
        P("mp"),
        P("mp"),
        P(None, "mp"),
        P("dp", None),
        P(),
        P("dp", None),
    )
    return jax.shard_map(
        shards,
        mesh=mesh,
        in_specs=placed,
        out_specs=(
            P("dp", "mp"),
            P("dp", None, "mp"),
            P("dp", "mp"),
            P(None, "mp"),
            P("mp"),
            P("mp"),
        ),
        check_vma=False,
    )
```

profile of v0, /device:TPU:4, one launch (start us, length us, event | category | flops | bytes accessed | tf_op | source)
XLA Modules:
  0.0 1084.7 jit_solution(16203160187497668343)
XLA Ops:
  17.8 1.6 fusion.78
  19.4 1.7 fusion.77
  21.0 1.4 reduce_sum.335
  22.4 1.2 dynamic_slice.3
  24.2 1.4 copy.25
  32.0 0.9 fusion.62
  39.0 0.9 fusion.14
  40.1 0.9 fusion.13
  41.1 6.2 multiply_reduce_fusion.32
  47.6 258.3 %all-reduce.89 = (f32[256]{0:T(256)S(1)}, f32[256]{0:T(256)S(1)}) all-reduce(f32[256]{0:T(256)} %get-tuple-element.58, f32[256]{0:T(256)S(1)} %get-tuple-element.57), channel_id=1, replica_groups=mesh['dp'=128,'mp'=4] {'dp'}, use_global_device_ids=true, to_apply=%region_6.7 | all-reduce | flops 512 | bytes 4096 | tf_op jit(solution)/shard_map/psum | solution.py:50
  306.0 2.3 fusion.46
  308.3 247.3 %all-reduce.88 = (f32[256]{0:T(256)}, f32[256]{0:T(256)S(1)}) all-reduce(f32[256]{0:T(256)S(1)} %get-tuple-element.56, f32[256]{0:T(256)S(1)} %get-tuple-element.55), channel_id=1, replica_groups=mesh['dp'=128,'mp'=4] {'dp'}, use_global_device_ids=true, to_apply=%region_10.11 | all-reduce | flops 512 | bytes 4096 | tf_op jit(solution)/shard_map/psum | solution.py:64
  556.2 2.9 multiply_reduce_fusion
  560.5 1.5 convolution_bitcast_fusion.1
  562.3 3.4 multiply_convert_fusion.2
  567.0 1.9 pad_maximum_fusion
  568.9 3.5 copy.21
  572.5 2.3 convolution_convert_fusion
  574.8 2.3 multiply_reduce_fusion.27
  577.2 2.5 multiply_reduce_fusion.18
  579.7 1.1 multiply_reduce_fusion.9
  580.9 2.8 stack.127
  583.7 491.3 %psum.39 = f32[31,256]{1,0:T(8,128)} all-reduce(f32[31,256]{1,0:T(8,128)S(1)} %stack.127), channel_id=1, replica_groups=mesh['dp'=128,'mp'=4] {'dp'}, use_global_device_ids=true, to_apply=%region_44.45 | all-reduce | flops 7936 | bytes 63488 | tf_op jit(solution)/shard_map/psum | solution.py:76
  1076.6 1.3 slice.684
  (234 shorter events, 26.9 us)
Async XLA Ops:
  7.2 18.5 %copy-start = (bf16[256,1024]{1,0:T(8,128)(2,1)S(1)}, bf16[256,1024]{1,0:T(8,128)(2,1)}, u32[]{:S(2)}) copy-start(bf16[256,1024]{1,0:T(8,128)(2,1)} %param.9) | copy-start | bytes 1572868
  7.2 1067.8 %reduce-scatter.7.cloned.1.call-start = ((), (), s32[]{:S(2)}) async-start(), calls=%async_computation.3 | async-start | bytes 3170304
  38.4 9.0 copy-start.1
  39.9 7.4 copy-start.28
  39.9 7.4 copy-start.30
  40.0 7.4 copy-start.33
  40.0 7.4 copy-start.36
  40.0 7.4 copy-start.38
  40.0 7.4 copy-start.40
  40.0 7.4 copy-start.42
  40.0 7.4 copy-start.44
  40.0 7.4 copy-start.46
  40.0 7.4 copy-start.48
  40.0 7.4 copy-start.50
  40.0 7.4 copy-start.52
  40.1 7.4 copy-start.54
  40.1 7.4 copy-start.56
  41.0 6.5 copy-start.16
  41.0 6.5 copy-start.18
  305.9 249.7 %copy-start.84 = (f32[256]{0:T(256)}, f32[256]{0:T(256)S(1)}, u32[]{:S(2)}) copy-start(f32[256]{0:T(256)S(1)} %get-tuple-element.67) | copy-start | bytes 3076
  305.9 253.2 %copy-start.83 = (f32[256]{0:T(256)}, f32[256]{0:T(256)S(1)}, u32[]{:S(2)}) copy-start(f32[256]{0:T(256)S(1)} %get-tuple-element.66) | copy-start | bytes 3076
  572.4 7.3 copy-start.3
  572.4 7.3 copy-start.32
  572.4 505.5 %reduce-scatter.5.cloned.1.call-start = ((), (), s32[]{:S(2)}) async-start(), calls=%async_computation.2 | async-start | bytes 655360 | tf_op jit(solution)/shard_map/reduce_scatter | solution.py:90
  (64 other events, 216.2 us)
Sparse Core Ops, SparseCore 0:
  572.5 194.4 reduce-scatter.6
  770.4 22.4 reduce-scatter.4
where the time goes:
time: 1090 us; the launch traced here: 1080 us
  blocking collectives  997 us (91%)
  local copies, waits for them, and re-layouts  39.2 us (4%)
  other arithmetic  24.7 us (2%)
  between operations  16.7 us (2%)
    psum x1, blocking collectives, shards(): depth_grad = lax.psum(jnp.stack(depth_rows), 'dp')  491 us
    psum x1, blocking collectives, shards(): lax.psum((jnp.sum(conv_out, axis=0), jnp.sum(conv_out * conv_out, axis=0)...  258 us
    psum x1, blocking collectives, shards(): shift_grad, gain_grad = lax.psum((local_shift, local_gain), 'dp')  247 us
  transfers between devices with their start and end apart: 2, of which 0 were waited for; matrix products, arithmetic and copies ran while one was open for 1% of the time, Pallas kernels for 0%

commit v1 on v0

--- a/solution.py
+++ b/solution.py
@@ -73,7 +73,7 @@
         depth_rows.append(
             jnp.sum(grad_conv * tap_term(glu_float, owner_id, live_col, tap_index - radius), axis=0)
         )
-    depth_grad = lax.psum(jnp.stack(depth_rows), "dp")
+    depth_grad = jnp.sum(lax.all_gather(jnp.stack(depth_rows), "dp"), axis=0)
     grad_glu = jnp.zeros((frames_dev, channels), jnp.float32)
     for tap_index in range(tap_count):
         offset = tap_index - radius

time: 1090 us -> 887 us (0.81)
  the two profiles are of different devices: /device:TPU:4 before, /device:TPU:8 now
where the time goes in v1:
time: 887 us; the launch traced here: 886 us
  blocking collectives  470 us (53%)
  waiting for transfers between devices  323 us (36%)
  local copies, waits for them, and re-layouts  41.4 us (5%)
  other arithmetic  27.8 us (3%)
  between operations  16.5 us (2%)
    psum x1, blocking collectives, shards(): shift_grad, gain_grad = lax.psum((local_shift, local_gain), 'dp')  247 us
    psum x1, blocking collectives, shards(): lax.psum((jnp.sum(conv_out, axis=0), jnp.sum(conv_out * conv_out, axis=0)...  223 us
    unnamed x4, waiting for transfers between devices  216 us
    all_gather x1, waiting for transfers between devices, shards(): depth_grad = jnp.sum(lax.all_gather(jnp.stack(depth_rows), 'dp'), axis=0)  82.4 us
    reduce_scatter x1, waiting for transfers between devices, shards(): lax.psum_scatter(frame_term.astype(jnp.bfloat16), 'mp', scatter_dimension...  24.6 us
    slice x29, local copies, waits for them, and re-layouts, time_shift(): return jnp.concatenate([pad_part, values[:offset]], axis=0)  20.8 us
  transfers between devices with their start and end apart: 3, of which 3 were waited for; matrix products, arithmetic and copies ran while one was open for 2% of the time, Pallas kernels for 0%

profile of v1, /device:TPU:8, one launch (start us, length us, event | category | flops | bytes accessed | tf_op | source)
XLA Modules:
  0.0 885.7 jit_solution(5260216377612932720)
XLA Ops:
  17.6 1.6 fusion.78
  19.2 1.7 fusion.77
  20.9 1.4 reduce_sum.344
  22.3 1.2 dynamic_slice.3
  24.1 1.4 copy.25
  40.9 6.2 multiply_reduce_fusion.32
  47.4 222.9 %all-reduce.89 = (f32[256]{0:T(256)S(1)}, f32[256]{0:T(256)S(1)}) all-reduce(f32[256]{0:T(256)} %get-tuple-element.58, f32[256]{0:T(256)S(1)} %get-tuple-element.57), channel_id=1, replica_groups=mesh['dp'=128,'mp'=4] {'dp'}, use_global_device_ids=true, to_apply=%region_6.7 | all-reduce | flops 512 | bytes 4096 | tf_op jit(solution)/shard_map/psum | solution.py:50
  270.3 2.3 fusion.46
  272.6 247.4 %all-reduce.88 = (f32[256]{0:T(256)}, f32[256]{0:T(256)S(1)}) all-reduce(f32[256]{0:T(256)S(1)} %get-tuple-element.56, f32[256]{0:T(256)S(1)} %get-tuple-element.55), channel_id=1, replica_groups=mesh['dp'=128,'mp'=4] {'dp'}, use_global_device_ids=true, to_apply=%region_10.11 | all-reduce | flops 512 | bytes 4096 | tf_op jit(solution)/shard_map/psum | solution.py:64
  520.5 2.9 multiply_reduce_fusion
  524.8 1.5 convolution_bitcast_fusion.1
  526.7 3.4 multiply_convert_fusion.2
  531.3 1.9 pad_maximum_fusion
  533.2 3.6 copy.21
  536.9 2.3 multiply_reduce_fusion.27
  539.2 2.5 multiply_reduce_fusion.18
  541.8 1.1 multiply_reduce_fusion.9
  542.9 5.2 stack.127
  548.3 2.2 convolution_convert_fusion
  550.5 215.7 %reduce-scatter.7.cloned.1.call-done = f32[8,768]{1,0:T(8,128)} async-done(((f32[1024,768]{1,0:T(8,128)}), f32[8,768]{1,0:T(8,128)}) %reduce-scatter.7.cloned.1.call-update) | async-done | bytes 24592
  767.8 1.3 slice.684
  769.1 82.4 %all-gather.4.cloned.1.call-done = f32[128,31,256]{2,1,0:T(8,128)} async-done(((f32[1,31,256]{2,1,0:T(8,128)}), f32[128,31,256]{2,1,0:T(8,128)}) %all-gather.4.cloned.1.call-update) | async-done | bytes 4063248 | tf_op jit(solution)/shard_map/all_gather | solution.py:76
  851.5 3.1 reduce_sum.379
  854.6 24.6 %reduce-scatter.5.cloned.1.call-done = bf16[256,256]{1,0:T(8,128)(2,1)} async-done(((bf16[256,1024]{1,0:T(8,128)(2,1)}), bf16[256,256]{1,0:T(8,128)(2,1)}) %reduce-scatter.5.cloned.1.call-update) | async-done | bytes 131088 | tf_op jit(solution)/shard_map/reduce_scatter | solution.py:90
  (237 shorter events, 29.4 us)
Async XLA Ops:
  7.2 18.4 %copy-start = (bf16[256,1024]{1,0:T(8,128)(2,1)S(1)}, bf16[256,1024]{1,0:T(8,128)(2,1)}, u32[]{:S(2)}) copy-start(bf16[256,1024]{1,0:T(8,128)(2,1)} %param.9) | copy-start | bytes 1572868
  7.2 759.0 %reduce-scatter.7.cloned.1.call-start = ((), (), s32[]{:S(2)}) async-start(), calls=%async_computation.4 | async-start | bytes 3170304
  38.2 9.0 %copy-start.1 = (f32[253,256]{1,0:T(8,128)}, f32[253,256]{1,0:T(8,128)S(1)}, u32[]{:S(2)}) copy-start(f32[253,256]{1,0:T(8,128)S(1)} %get-tuple-element.123) | copy-start | bytes 777220
  39.7 7.4 copy-start.28
  39.8 7.4 copy-start.30
  39.8 7.4 copy-start.33
  39.8 7.4 copy-start.36
  39.8 7.4 copy-start.38
  39.8 7.4 copy-start.40
  39.8 7.4 copy-start.42
  39.8 7.4 copy-start.44
  39.8 7.4 copy-start.46
  39.8 7.4 copy-start.48
  39.8 7.4 copy-start.50
  39.9 7.4 copy-start.52
  39.9 7.4 copy-start.54
  39.9 7.4 copy-start.56
  40.8 6.5 copy-start.14
  40.8 6.5 copy-start.16
  40.8 6.5 copy-start.18
  270.3 249.7 %copy-start.84 = (f32[256]{0:T(256)}, f32[256]{0:T(256)S(1)}, u32[]{:S(2)}) copy-start(f32[256]{0:T(256)S(1)} %get-tuple-element.67) | copy-start | bytes 3076
  270.3 253.2 %copy-start.83 = (f32[256]{0:T(256)}, f32[256]{0:T(256)S(1)}, u32[]{:S(2)}) copy-start(f32[256]{0:T(256)S(1)} %get-tuple-element.66) | copy-start | bytes 3076
  536.8 314.7 %all-gather.4.cloned.1.call-start = ((), (), s32[]{:S(2)}) async-start(), calls=%async_computation.3 | async-start | bytes 4227072 | tf_op jit(solution)/shard_map/all_gather | solution.py:76
  548.2 330.9 %reduce-scatter.5.cloned.1.call-start = ((), (), s32[]{:S(2)}) async-start(), calls=%async_computation.2 | async-start | bytes 655360 | tf_op jit(solution)/shard_map/reduce_scatter | solution.py:90
  (65 other events, 215.2 us)
Sparse Core Ops, SparseCore 0:
  536.9 229.2 reduce-scatter.6
  769.9 81.5 all-gather.3
  854.9 24.2 reduce-scatter.4
